TPU v7x, 512 devices: a whole 4x8x8 slice. The times are simulated.
512 devices in a mesh: row: 16 (over z, core), col: 32 (over y, x).
Axes of the slice: x: 4, y: 8, z: 8, core: 2. Of those that a mesh axis runs over, the one named last changes fastest.
Arguments:
- initial_voltage: float32 [16, 64, 128, 128], P('row', 'col'), may hold values from -6 to 6
- inject: float32 [16, 64, 128, 128], P('row', 'col'), may hold values from -6 to 6
- conduct: float32 [16, 64, 128, 128], P('row', 'col'), as said below
- capacitance: float32 [16, 64, 128], P('row', 'col'), may hold values from 1 to 4
- track_gain: float32 [16, 64, 2, 32], P('row', 'col'), may hold values from 0.3 to 3
- driver_tile: int32 [16, 32, 64], P('row', 'col'), may hold values from 0 to 1
- sink_net: int32 [16, 32, 32, 8], P('row', 'col'), may hold values from 0 to 63
- sink_count: int32 [16, 32, 32], P('row', 'col'), may hold values from 0 to 8, as said below
- sink_tile: int32 [16, 32, 32, 8], P('row', 'col'), may hold values from 0 to 1
- sink_node: int32 [16, 32, 32, 8], P('row', 'col'), may hold values from 0 to 127
- sink_gain: float32 [16, 32, 32, 8], P('row', 'col'), may hold values from 0.5 to 2
Outputs:
- voltage: float32 [16, 64, 128, 128], P('row', 'col')
Inputs may be any that keep to these rules, and one draw needn't show every extreme that they name: Slots k >= sink_count[d, s] are ignored; some receiving device takes all 8 slots from some source device in every draw. `conduct`: each tile's block is symmetric with non-positive entries off the diagonal and rows summing to zero.
All inputs are finite; a program needn't handle non-finite values.
Results may differ from a plain program's by a relative error of at most 0.0001.
Values sent between devices are 32-bit elements; how exact they have to be, the bound alone decides.
A program may use at most 64 MiB of HBM per device.

v0:
```python
import jax
import jax.numpy as jnp
from jax import lax
from jax.sharding import PartitionSpec as P

ITERS = 3


PRECISE = lax.Precision.HIGHEST


def padded_2(block, sides, width):
    for axis, dim in sides:
        count = lax.axis_size(axis)
        forward = [(i, i + 1) for i in range(count - 1)]
        backward = [(target, source) for source, target in forward]
        low = lax.ppermute(
            lax.slice_in_dim(block, block.shape[dim] - width, None, axis=dim), axis, forward
        )
        high = lax.ppermute(lax.slice_in_dim(block, 0, width, axis=dim), axis, backward)
        block = jnp.concatenate([low, block, high], axis=dim)
    return block


def shifted(block, axis, distance):
    devices = range(lax.axis_size(axis))
    route = [(i - distance, i) for i in devices if i - distance in devices]
    return lax.ppermute(block, axis, route)


def tile_inverse(conduct, capacitance):
    node_count = conduct.shape[-1]
    identity = jnp.eye(node_count, dtype=jnp.float32)
    whole_block = conduct + capacitance[..., None] * identity
    flat_blocks = whole_block.reshape((-1, node_count, node_count))
    factors = jnp.linalg.cholesky(flat_blocks)
    inverse = jax.vmap(lambda factor: jax.scipy.linalg.cho_solve((factor, True), identity))(factors)
    return inverse.reshape(whole_block.shape)


def apply_grid(voltage, conduct, capacitance, track_pad):
    edge_count = track_pad.shape[-1]
    inner_part = (
        jnp.einsum("rcij,rcjp->rcip", conduct, voltage, precision=PRECISE)
        + capacitance[..., None] * voltage
    )
    rim_cells = voltage[:, :, :edge_count, :]
    padded = padded_2(rim_cells, (("row", 0), ("col", 1)), 1)
    east_gain = track_pad[1:-1, 1:-1, 0][..., None]
    west_gain = track_pad[1:-1, :-2, 0][..., None]
    south_gain = track_pad[1:-1, 1:-1, 1][..., None]
    north_gain = track_pad[:-2, 1:-1, 1][..., None]
    track_flow = east_gain * (rim_cells - padded[1:-1, 2:]) + west_gain * (
        rim_cells - padded[1:-1, :-2]
    )
    track_flow = (
        track_flow
        + south_gain * (rim_cells - padded[2:, 1:-1])
        + north_gain * (rim_cells - padded[:-2, 1:-1])
    )
    return jnp.concatenate(
        [inner_part[:, :, :edge_count] + track_flow, inner_part[:, :, edge_count:]], axis=2
    )


def precondition(inverse, residual):
    return jnp.einsum("rcij,rcjp->rcip", inverse, residual, precision=PRECISE)


def inner_sum(left_vec, right_vec):
    return jnp.sum(left_vec * right_vec, axis=(0, 1, 2))


def residual_product(residual, precond):
    return lax.psum(inner_sum(residual, precond), ("row", "col"))


def solve_separate(right_side, initial, conduct, capacitance, track_pad, inverse):
    solution = initial
    residual = right_side - apply_grid(initial, conduct, capacitance, track_pad)
    precond = precondition(inverse, residual)
    direction = precond
    rz_now = residual_product(residual, precond)
    for sweep_idx in range(ITERS):
        applied = apply_grid(direction, conduct, capacitance, track_pad)
        curvature = lax.psum(inner_sum(direction, applied), ("row", "col"))
        step_size = rz_now / curvature
        solution = solution + step_size * direction
        residual = residual - step_size * applied
        precond = precondition(inverse, residual)
        rz_fresh = residual_product(residual, precond)
        direction = precond + rz_fresh / rz_now * direction
        rz_now = rz_fresh
    return solution


def driver_voltage(voltage, driver_tile):
    node_count = voltage.shape[2]
    flat_field = voltage.reshape((-1, voltage.shape[3]))
    net_count = driver_tile.shape[-1]
    row_index = (
        driver_tile.reshape(-1) * node_count + jnp.arange(net_count, dtype=jnp.int32) % node_count
    )
    return jnp.take(flat_field, row_index, axis=0)


def sink_current(values, sink_tile, sink_node, sink_gain, sink_count, node_count, tile_count):
    source_count, slot_count, pattern_count = values.shape
    live_slot = jnp.arange(slot_count, dtype=jnp.int32)[None, :] < sink_count.reshape(
        (source_count, 1)
    )
    weight = jnp.where(live_slot, sink_gain.reshape((source_count, slot_count)), jnp.float32(0.0))
    row_index = (sink_tile * node_count + sink_node).reshape(-1)
    scaled = (values * weight[..., None]).reshape((-1, pattern_count))
    injected = jnp.zeros((tile_count * node_count, pattern_count), jnp.float32)
    return injected.at[row_index].add(scaled)


def lower_rims(track_gain):
    west_piece = shifted(track_gain[:, -1:, 0, :], "col", 1)
    north_piece = shifted(track_gain[-1:, :, 1, :], "row", 1)
    track_pad = jnp.pad(track_gain, ((1, 1), (1, 1), (0, 0), (0, 0)))
    track_pad = track_pad.at[1:-1, 0, 0].set(west_piece[:, 0])
    return track_pad.at[0, 1:-1, 1].set(north_piece[0])


def local(
    initial_voltage,
    inject,
    conduct,
    capacitance,
    track_gain,
    driver_tile,
    sink_net,
    sink_count,
    sink_tile,
    sink_node,
    sink_gain,
):
    inverse = tile_inverse(conduct, capacitance)
    track_pad = lower_rims(track_gain)
    col_count = lax.axis_size("col")
    net_count = driver_tile.shape[-1]
    pattern_count = initial_voltage.shape[3]
    node_count = initial_voltage.shape[2]
    tile_count = initial_voltage.shape[0] * initial_voltage.shape[1]
    wanted = sink_net.reshape((sink_net.shape[2], sink_net.shape[3]))
    voltage = initial_voltage
    drivers = driver_voltage(voltage, driver_tile)
    gathered = lax.all_gather(drivers, "col", axis=0, tiled=True)
    offsets = jnp.arange(col_count, dtype=jnp.int32)[:, None] * net_count
    values = jnp.take(gathered, (wanted + offsets).reshape(-1), axis=0).reshape(
        wanted.shape + (pattern_count,)
    )
    injected = sink_current(
        values, sink_tile, sink_node, sink_gain, sink_count, node_count, tile_count
    )
    right_side = capacitance[..., None] * voltage + inject + injected.reshape(voltage.shape)
    voltage = solve_separate(right_side, voltage, conduct, capacitance, track_pad, inverse)
    return voltage


def solution(mesh):
    placed = (
        P("row", "col", None, None),
        P("row", "col", None, None),
        P("row", "col", None, None),
        P("row", "col", None),
        P("row", "col", None, None),
        P("row", "col", None),
        P("row", "col", None, None),
        P("row", "col", None),
        P("row", "col", None, None),
        P("row", "col", None, None),
        P("row", "col", None, None),
    )
    return jax.shard_map(
        local, mesh=mesh, in_specs=placed, out_specs=P("row", "col", None, None), check_vma=False
    )
```

profile of v0, /device:TPU:1, one launch (start us, length us, event | category | flops | bytes accessed | tf_op | source)
XLA Modules:
  0.0 707.5 jit_solution(17942465035946714458)
XLA Ops:
  7.6 8.8 %collective-permute-start.2 = (f32[1,2,32,128]{2,3,1,0:T(8,128)S(1)}, f32[1,2,32,128]{2,3,1,0:T(8,128)S(1)}, u32[]{:S(2)}, u32[]{:S(2)}) collective-permute-start(f32[1,2,32,128]{2,3,1,0:T(8,128)S(1)} %bitcast.150), channel_id=1, source_target_pairs={{32,0},{64,32},{96,64},{128,96},{160,128},{192,160},{224,192},{256... | collective-permute-start | bytes 98312 | tf_op jit(solution)/shard_map/ppermute | solution.py:20
  16.4 1.9 collective-permute-start.1
  19.7 1.9 collective-permute-start.5
  29.1 1.3 collective-permute-start.3
  30.4 4.0 collective-permute-start.4
  35.9 66.4 %all-gather.2.cloned.1.call-done = f32[2048,128]{1,0:T(8,128)} async-done(((f32[64,128]{1,0:T(8,128)}), f32[2048,128]{1,0:T(8,128)}) %all-gather.2.cloned.1.call-update) | async-done | bytes 1048592 | tf_op jit(solution)/shard_map/all_gather | solution.py:150
  102.3 3.4 scatter_custom_fusion
  106.0 23.5 %custom-call.11 = f32[2,128,128]{2,1,0:T(8,128)S(1)} custom-call(f32[2,128,128]{2,1,0:T(8,128)S(1)} %fusion.13), custom_call_target="Cholesky" | custom-call | tf_op jit(solution)/shard_map/jit(cholesky)/cholesky | solution.py:36
  129.8 19.7 %custom-call.12 = f32[2,1,128,128]{2,3,1,0:T(8,128)S(1)} custom-call(f32[2,1,128,128]{3,2,1,0:T(8,128)S(1)} %select_bitcast_fusion), custom_call_target="InvertDiagBlocksLowerTriangular" | custom-call | tf_op jit(solution)/shard_map/vmap(jit(_cho_solve))/triangular_solve | solution.py:37
  151.0 6.9 collective-permute-start.7
  157.9 3.2 collective-permute-start.6
  164.4 4.0 collective-permute-start.9
  170.1 103.8 %all-reduce.1 = (f32[128]{0:T(128)S(1)}, f32[128]{0:T(128)S(1)}) all-reduce(f32[128]{0:T(128)S(1)} %multiply_reduce_fusion, f32[128]{0:T(128)S(1)} %fusion.8), channel_id=1, replica_groups=mesh['row'=16,'col'=32] {'row','col'}, use_global_device_ids=true, to_apply=%region_4.5 | all-reduce | flops 256 | bytes 2048 | tf_op jit(solution)/shard_map/psum | solution.py:75
  274.5 95.4 %psum.44 = f32[128]{0:T(128)S(1)} all-reduce(f32[128]{0:T(128)S(1)} %get-tuple-element.56), channel_id=1, replica_groups=mesh['row'=16,'col'=32] {'row','col'}, use_global_device_ids=true, to_apply=%region_8.9 | all-reduce | flops 128 | bytes 1024 | tf_op jit(solution)/shard_map/psum | solution.py:75
  370.0 2.6 collective-permute-start.11
  372.6 3.3 collective-permute-start.10
  379.2 4.0 collective-permute-start.13
  384.8 102.0 %psum.45 = f32[128]{0:T(128)S(1)} all-reduce(f32[128]{0:T(128)S(1)} %fusion.10), channel_id=1, replica_groups=mesh['row'=16,'col'=32] {'row','col'}, use_global_device_ids=true, to_apply=%region_10.11 | all-reduce | flops 128 | bytes 1024 | tf_op jit(solution)/shard_map/psum | solution.py:86
  487.4 95.3 %psum.46 = f32[128]{0:T(128)S(1)} all-reduce(f32[128]{0:T(128)S(1)} %get-tuple-element.58), channel_id=1, replica_groups=mesh['row'=16,'col'=32] {'row','col'}, use_global_device_ids=true, to_apply=%region_12.13 | all-reduce | flops 128 | bytes 1024 | tf_op jit(solution)/shard_map/psum | solution.py:75
  582.7 2.6 collective-permute-start.15
  585.3 3.5 collective-permute-start.14
  590.8 1.3 collective-permute-start.16
  592.1 4.0 collective-permute-start.17
  597.8 102.0 %psum.47 = f32[128]{0:T(128)S(1)} all-reduce(f32[128]{0:T(128)S(1)} %fusion.12), channel_id=1, replica_groups=mesh['row'=16,'col'=32] {'row','col'}, use_global_device_ids=true, to_apply=%region_14.15 | all-reduce | flops 128 | bytes 1024 | tf_op jit(solution)/shard_map/psum | solution.py:86
  (152 shorter events, 28.8 us)
Async XLA Ops:
  6.5 15.1 %copy-start.1 = (f32[1,2,128,128]{3,2,1,0:T(8,128)S(1)}, f32[1,2,128,128]{3,2,1,0:T(8,128)}, u32[]{:S(2)}) copy-start(f32[1,2,128,128]{3,2,1,0:T(8,128)} %param.15) | copy-start | bytes 393220
  6.5 11.8 %copy-start.4 = (f32[1,2,2,32]{3,2,1,0:T(2,128)S(1)}, f32[1,2,2,32]{3,2,1,0:T(2,128)}, u32[]{:S(2)}) copy-start(f32[1,2,2,32]{3,2,1,0:T(2,128)} %param.19) | copy-start | bytes 1540
  6.5 95.8 %all-gather.2.cloned.1.call-start = ((), (), s32[]{:S(2)}) async-start(), calls=%async_computation | async-start | bytes 1081344 | tf_op jit(solution)/shard_map/all_gather | solution.py:150
  7.6 21.3 %collective-permute-start.2 = (f32[1,2,32,128]{2,3,1,0:T(8,128)S(1)}, f32[1,2,32,128]{2,3,1,0:T(8,128)S(1)}, u32[]{:S(2)}, u32[]{:S(2)}) collective-permute-start(f32[1,2,32,128]{2,3,1,0:T(8,128)S(1)} %bitcast.150), channel_id=1, source_target_pairs={{32,0},{64,32},{96,64},{128,96},{160,128},{192,160},{224,192},{256... | collective-permute-start | bytes 98312 | tf_op jit(solution)/shard_map/ppermute | solution.py:20
  16.4 12.6 %collective-permute-start.1 = (f32[1,2,32,128]{2,3,1,0:T(8,128)S(1)}, f32[1,2,32,128]{2,3,1,0:T(8,128)S(1)}, u32[]{:S(2)}, u32[]{:S(2)}) collective-permute-start(f32[1,2,32,128]{2,3,1,0:T(8,128)S(1)} %bitcast.151), channel_id=1, source_target_pairs={{0,32},{32,64},{64,96},{96,128},{128,160},{160,192},{192,224},{224... | collective-permute-start | bytes 98312 | tf_op jit(solution)/shard_map/ppermute | solution.py:17
  18.4 10.5 %collective-permute-start = (f32[1,1,32]{2,1,0:T(1,128)S(1)}, f32[1,1,32]{2,1,0:T(1,128)S(1)}, u32[]{:S(2)}, u32[]{:S(2)}) collective-permute-start(f32[1,1,32]{2,1,0:T(1,128)S(1)} %slice_bitcast_fusion.1), channel_id=1, source_target_pairs={{0,1},{1,2},{2,3},{3,4},{4,5},{5,6},{6,7},{7,8},{8,9},{9,10},{10,1... | collective-permute-start | bytes 392 | tf_op jit(solution)/shard_map/ppermute | solution.py:28
  19.7 1.9 copy-start.10
  19.7 16.1 %collective-permute-start.5 = (f32[1,2,32]{2,1,0:T(2,128)S(1)}, f32[1,2,32]{2,1,0:T(2,128)S(1)}, u32[]{:S(2)}, u32[]{:S(2)}) collective-permute-start(f32[1,2,32]{2,1,0:T(2,128)S(1)} %bitcast.184), channel_id=1, source_target_pairs={{0,32},{32,64},{64,96},{96,128},{128,160},{160,192},{192,224},{224... | collective-permute-start | bytes 776 | tf_op jit(solution)/shard_map/ppermute | solution.py:28
  23.8 2.7 copy-start
  27.9 0.9 copy-start.2
  29.1 5.3 collective-permute-start.3
  30.4 5.2 collective-permute-start.4
  151.0 10.8 %collective-permute-start.7 = (f32[1,2,32,128]{2,3,1,0:T(8,128)S(1)}, f32[1,2,32,128]{2,3,1,0:T(8,128)S(1)}, u32[]{:S(2)}, u32[]{:S(2)}) collective-permute-start(f32[1,2,32,128]{2,3,1,0:T(8,128)S(1)} %bitcast.142), channel_id=1, source_target_pairs={{32,0},{64,32},{96,64},{128,96},{160,128},{192,160},{224,192},{256... | collective-permute-start | bytes 98312 | tf_op jit(solution)/shard_map/ppermute | solution.py:20
  157.9 5.1 collective-permute-start.6
  163.1 5.4 collective-permute-start.8
  164.4 5.2 collective-permute-start.9
  370.0 6.6 collective-permute-start.11
  372.6 5.2 collective-permute-start.10
  377.9 5.4 collective-permute-start.12
  379.2 5.2 collective-permute-start.13
  582.7 6.8 collective-permute-start.15
  585.3 5.4 collective-permute-start.14
  590.8 5.4 collective-permute-start.16
  592.1 5.2 collective-permute-start.17
  (6 other events, 4.1 us)
Sparse Core Ops, SparseCore 0:
  23.1 79.1 all-gather.1
where the time goes:
time: 709 us; the launch traced here: 707 us
  blocking collectives  498 us (70%)
  waiting for transfers between devices  75.2 us (11%)
  starting transfers between devices  57.1 us (8%)
  other arithmetic  49.2 us (7%)
  between operations  14.1 us (2%)
  local copies, waits for them, and re-layouts  9.8 us (1%)
    psum x3, blocking collectives, residual_product(): return lax.psum(inner_sum(residual, precond), ('row', 'col'))  294 us
    psum x2, blocking collectives, solve_separate(): curvature = lax.psum(inner_sum(direction, applied), ('row', 'col'))  204 us
    all_gather x1, waiting for transfers between devices, local(): gathered = lax.all_gather(drivers, 'col', axis=0, tiled=True)  66.4 us
    ppermute x8, starting transfers between devices, padded_2(): lax.ppermute(lax.slice_in_dim(block, block.shape[dim] - width, None, axis...  27.8 us
    ppermute x8, starting transfers between devices, padded_2(): lax.ppermute(lax.slice_in_dim(block, 0, width, axis=dim), axis, backward)  26 us
    another operation x4, other arithmetic, tile_inverse(): factors = jnp.linalg.cholesky(flat_blocks)  23.6 us
    another operation x3, other arithmetic, tile_inverse(): jax.scipy.linalg.cho_solve((factor, True), identity)  19.8 us
  transfers between devices with their start and end apart: 19, of which 11 were waited for; matrix products, arithmetic and copies ran while one was open for 1% of the time, Pallas kernels for 0%

commit v1 on v0

v1 whole, which is shorter than its diff:
```python
import functools

import jax
import jax.numpy as jnp
from jax import lax
from jax.experimental import pallas as pl
from jax.experimental.pallas import tpu as pltpu
from jax.sharding import PartitionSpec as P

F32 = jnp.float32
HIGH = lax.Precision.HIGHEST
MESH = pl.DeviceIdType.MESH
SCALE = 1.0 / 32.0
PIVOTS = 4


def dot(left, right):
    return jnp.dot(left, right, precision=HIGH, preferred_element_type=F32)


def lane_splat(block, lane):
    return jnp.take_along_axis(block, jnp.full(block.shape, lane, jnp.int32), axis=1)


def pivot_rows(rows, first, offset, lane):
    mine = [rows[offset + i : offset + i + 1] for i in range(PIVOTS)]
    splats = [lane_splat(rows, first + j) for j in range(PIVOTS)]
    small = [
        [splats[j][offset + i : offset + i + 1] for j in range(PIVOTS)]
        for i in range(PIVOTS)
    ]
    for j in range(PIVOTS):
        scale = 1.0 / small[j][j]
        row = [scale if m == j else small[j][m] * scale for m in range(PIVOTS)]
        for i in range(PIVOTS):
            if i == j:
                continue
            factor = small[i][j]
            small[i] = [
                -factor * scale if m == j else small[i][m] - factor * row[m]
                for m in range(PIVOTS)
            ]
        small[j] = row
    fresh = []
    for i in range(PIVOTS):
        total = small[i][0] * mine[0]
        for j in range(1, PIVOTS):
            total = total + small[i][j] * mine[j]
        for j in range(PIVOTS):
            total = jnp.where(lane == first + j, small[i][j], total)
        fresh.append(total)
    return fresh


def eliminate(mats, start, stop):
    nodes = mats[0].shape[0]
    lane = lax.broadcasted_iota(jnp.int32, (1, nodes), 1)

    def group(index, carry):
        base = pl.multiple_of(index * 8, 8)
        for offset in range(0, 8, PIVOTS):
            first = base + offset
            whole = [mat[...] for mat in mats]
            rows = [mat[pl.ds(base, 8), :] for mat in mats]
            fresh = [pivot_rows(r, first, offset, lane) for r in rows]
            kept = (lane >= first) & (lane < first + PIVOTS)
            done = []
            for t in range(len(mats)):
                total = jnp.where(kept, 0.0, whole[t])
                for j in range(PIVOTS):
                    total = total - lane_splat(whole[t], first + j) * fresh[t][j]
                done.append(total)
            for t, mat in enumerate(mats):
                mat[...] = done[t]
                for j in range(PIVOTS):
                    mat[pl.ds(first + j, 1), :] = fresh[t][j]
        return carry

    lax.fori_loop(start, stop, group, 0)


def track_flow(fields, east, west, south, north, gains):
    one, two = fields
    gain_e0, gain_e1, gain_w, gain_s0, gain_s1, gain_n0, gain_n1 = gains
    half = one.shape[0]
    middle = gain_e0 * (one - two)
    flow_one = (
        middle
        + gain_w * (one - west)
        + gain_s0 * (one - south[:half])
        + gain_n0 * (one - north[:half])
    )
    flow_two = (
        gain_e1 * (two - east)
        - middle
        + gain_s1 * (two - south[half:])
        + gain_n1 * (two - north[half:])
    )
    return flow_one, flow_two


def column_sum(left, right):
    return jnp.sum(left * right, axis=0, keepdims=True)


def safe_inverse(value):
    return jnp.where(value > 0.0, 1.0 / value, 0.0)


def combination(n):
    up = 1.0 / SCALE
    h00, h01, h02 = n[0] + up * n[1], n[1] + up * n[2], n[2] + up * n[3]
    h11, h12, h22 = h02, n[3] + up * n[4], n[4] + up * n[5]
    inv0 = safe_inverse(h00)
    l10, l20 = h01 * inv0, h02 * inv0
    d11, d12, d22 = h11 - l10 * h01, h12 - l10 * h02, h22 - l20 * h02
    g1, g2 = n[1] - l10 * n[0], n[2] - l20 * n[0]
    inv1 = safe_inverse(d11)
    l21 = d12 * inv1
    c2 = (g2 - l21 * g1) * safe_inverse(d22 - l21 * d12)
    c1 = (g1 - d12 * c2) * inv1
    c0 = (n[0] - h01 * c1 - h02 * c2) * inv0
    return c0, c1, c2


def kernel(
    sizes,
    volt,
    inject,
    conduct,
    cap,
    track,
    driver_tile,
    sink_net,
    sink_count,
    sink_tile,
    sink_node,
    sink_gain,
    out,
    mat0,
    mat1,
    ask,
    asked,
    give,
    given,
    stage0,
    halo0,
    stage,
    halo,
    *rest,
):
    n_row, n_col, rounds = sizes
    reduce_bufs = rest[: len(rounds)]
    ask_send, ask_recv, give_send, give_recv, halo_send, halo_recv, sum_send, sum_recv = rest[len(rounds) :]
    row, col = lax.axis_index("row"), lax.axis_index("col")
    nodes, edge = volt.shape[1], track.shape[1]
    slots = sink_net.shape[0]
    nets = driver_tile.shape[1]
    barrier = pltpu.get_barrier_semaphore()

    def row_peer(i):
        return (lax.rem(row + i, n_row), col)

    def col_peer(i):
        return (row, lax.rem(col + i, n_col))

    def greet(peer):
        def one(i, carry):
            pl.semaphore_signal(barrier, inc=1, device_id=peer(i), device_id_type=MESH)
            return carry

        return one

    lax.fori_loop(1, n_col, greet(col_peer), 0)
    lax.fori_loop(1, n_row, greet(row_peer), 0)

    wanted = sink_net[...].astype(F32)
    for s in range(n_col):
        ask[s * slots : (s + 1) * slots, :] = jnp.broadcast_to(
            wanted[:, s : s + 1], (slots, nodes)
        )
    stage0[0:edge, :] = volt[0, 0:edge, :]
    stage0[edge : 2 * edge, :] = volt[1, 0:edge, :]
    stage0[2 * edge : 2 * edge + 8, :] = jnp.zeros((8, nodes), F32)
    stage0[2 * edge : 2 * edge + 4, 0:edge] = track[...]

    pl.semaphore_wait(barrier, n_col + n_row - 2)

    def send_asks(i, carry):
        peer = col_peer(i)
        pltpu.make_async_remote_copy(
            src_ref=ask.at[pl.ds(pl.multiple_of(peer[1] * slots, slots), slots)],
            dst_ref=asked.at[pl.ds(pl.multiple_of(col * slots, slots), slots)],
            send_sem=ask_send,
            recv_sem=ask_recv,
            device_id=peer,
            device_id_type=MESH,
        ).start()
        return carry

    lax.fori_loop(1, n_col, send_asks, 0)

    neighbours = (col_peer(1), col_peer(n_col - 1), row_peer(1), row_peer(n_row - 1))

    def halo_copy(step, way):
        if step == 0:
            source, target = stage0, halo0.at[way]
        elif way == 0:
            source, target = stage.at[step - 1, 1], halo.at[step - 1, 0, 0]
        elif way == 1:
            source, target = stage.at[step - 1, 0], halo.at[step - 1, 1, 0]
        else:
            source, target = stage.at[step - 1], halo.at[step - 1, way]
        return pltpu.make_async_remote_copy(
            src_ref=source,
            dst_ref=target,
            send_sem=halo_send.at[step, way],
            recv_sem=halo_recv.at[step, way],
            device_id=neighbours[way],
            device_id_type=MESH,
        )

    for way in range(4):
        halo_copy(0, way).start()
    mine = pl.ds(pl.multiple_of(col * slots, slots), slots)
    asked[mine, :] = ask[mine, :]

    r_iota = lax.broadcasted_iota(jnp.int32, (nodes, nodes), 0)
    c_iota = lax.broadcasted_iota(jnp.int32, (nodes, nodes), 1)
    mats = (mat0, mat1)
    for t in range(2):
        mats[t][...] = conduct[t] + jnp.where(r_iota == c_iota, cap[t : t + 1, :], 0.0)
    groups = nodes // 8
    eliminate(mats, 0, groups // 2)

    lanes = lax.broadcasted_iota(jnp.int32, (1, 2 * nets), 1)
    tiles = jnp.concatenate([driver_tile[...], driver_tile[...]], axis=1)
    net_of = jnp.where(lanes >= nets, lanes - nets, lanes)
    tile_of = jnp.where(lanes >= nets, 1, 0)
    code = jnp.where(tiles == tile_of, net_of, -1).astype(F32)
    everything = pl.ds(0, (n_col - 1) * slots)
    pltpu.make_async_copy(asked.at[everything], asked.at[everything], ask_recv).wait()
    pick = jnp.where(asked[...] == code, 1.0, 0.0)
    give[...] = dot(pick, jnp.concatenate([volt[0, 0:nets, :], volt[1, 0:nets, :]], axis=0))

    def send_rows(i, carry):
        peer = col_peer(i)
        pltpu.make_async_remote_copy(
            src_ref=give.at[pl.ds(pl.multiple_of(peer[1] * slots, slots), slots)],
            dst_ref=given.at[pl.ds(pl.multiple_of(col * slots, slots), slots)],
            send_sem=give_send,
            recv_sem=give_recv,
            device_id=peer,
            device_id_type=MESH,
        ).start()
        return carry

    lax.fori_loop(1, n_col, send_rows, 0)
    given[mine, :] = give[mine, :]

    eliminate(mats, groups // 2, groups)

    slot_iota = lax.broadcasted_iota(jnp.int32, (slots, n_col), 0)
    weight = jnp.where(slot_iota < sink_count[...], sink_gain[...], 0.0)
    target = (sink_tile[...] * nodes + sink_node[...]).astype(F32)
    width = n_col * slots
    source = lax.broadcasted_iota(jnp.int32, (n_col, width), 0)
    place = lax.broadcasted_iota(jnp.int32, (n_col, width), 1)
    spread = jnp.where(place // slots == source, 1.0, 0.0)
    flat = dot(jnp.concatenate([target, weight], axis=0), spread)
    place = lax.broadcasted_iota(jnp.int32, (slots, width), 1)
    own = lax.rem(place, slots) == lax.broadcasted_iota(jnp.int32, (slots, width), 0)
    flat_target = jnp.sum(jnp.where(own, flat[:slots], 0.0), axis=0, keepdims=True)
    flat_weight = jnp.sum(jnp.where(own, flat[slots:], 0.0), axis=0, keepdims=True)
    node_row = lax.broadcasted_iota(jnp.int32, (2 * nodes, width), 0).astype(F32)
    scatter = jnp.where(node_row == flat_target, flat_weight, 0.0)

    base = [inject[t] - dot(conduct[t], volt[t]) for t in range(2)]

    for way in range(4):
        halo_copy(0, way).wait_recv()
    eye = lax.broadcasted_iota(jnp.int32, (edge, edge), 0) == lax.broadcasted_iota(
        jnp.int32, (edge, edge), 1
    )
    top = 2 * edge
    lines = [
        track[0:1, :],
        track[2:3, :],
        jnp.where(col == 0, 0.0, halo0[0, top + 2 : top + 3, 0:edge]),
        track[1:2, :],
        track[3:4, :],
        jnp.where(row == 0, 0.0, halo0[2, top + 1 : top + 2, 0:edge]),
        jnp.where(row == 0, 0.0, halo0[2, top + 3 : top + 4, 0:edge]),
    ]
    diagonal = jnp.concatenate([jnp.where(eye, line * SCALE, 0.0) for line in lines], axis=0)
    columns = dot(diagonal, jnp.ones((edge, nodes), F32))
    gains = [columns[i * edge : (i + 1) * edge] for i in range(7)]
    last_col, last_row = col == n_col - 1, row == n_row - 1

    def flow(fields, east, west, south, north):
        east = jnp.where(last_col, 0.0, east)
        south = jnp.where(last_row, 0.0, south)
        return track_flow(fields, east, west, south, north, gains)

    first_flow = flow(
        (volt[0, 0:edge, :], volt[1, 0:edge, :]),
        halo0[1, 0:edge, :],
        halo0[0, edge:top, :],
        halo0[3, 0:top, :],
        halo0[2, 0:top, :],
    )
    pltpu.make_async_copy(given.at[everything], given.at[everything], give_recv).wait()
    current = dot(scatter, given[...])
    resid, guess = [], []
    for t in range(2):
        total = base[t] + current[t * nodes : (t + 1) * nodes]
        total = jnp.concatenate(
            [total[:edge] - first_flow[t] * (1.0 / SCALE), total[edge:]], axis=0
        )
        resid.append(total)
        guess.append(dot(mats[t][...], total))

    moments = []
    fields = [guess[t][:edge] for t in range(2)]
    lifted = []
    for step in (1, 2, 3):
        for t in range(2):
            stage[step - 1, t] = fields[t]
        for way in range(4):
            halo_copy(step, way).start()
        if step == 1:
            moments.append(sum(column_sum(guess[t], resid[t]) for t in range(2)))
        else:
            moments.append(sum(column_sum(fields[t], flows[t]) for t in range(2)))
            lifted.append([dot(mats[t][:, 0:edge], flows[t]) for t in range(2)])
        for way in range(4):
            halo_copy(step, way).wait_recv()
        flows = flow(
            fields,
            halo[step - 1, 1, 0],
            halo[step - 1, 0, 0],
            halo[step - 1, 3].reshape(2 * edge, nodes),
            halo[step - 1, 2].reshape(2 * edge, nodes),
        )
        moments.append(sum(column_sum(fields[t], flows[t]) for t in range(2)))
        if step < 3:
            fields = [dot(mats[t][0:edge, 0:edge], flows[t]) for t in range(2)]

    total = jnp.concatenate(moments + [jnp.zeros((2, nodes), F32)], axis=0)
    for r, (axis, count, stride) in enumerate(rounds):
        buf = reduce_bufs[r]
        position = row if axis == 0 else col
        low = lax.rem(position, stride)
        slot = lax.rem(position // stride, count)
        high = position // (stride * count)
        buf[slot] = total

        def send_sum(i, carry):
            other = high * (stride * count) + lax.rem(slot + i, count) * stride + low
            pltpu.make_async_remote_copy(
                src_ref=buf.at[slot],
                dst_ref=buf.at[slot],
                send_sem=sum_send.at[r],
                recv_sem=sum_recv.at[r],
                device_id=(other, col) if axis == 0 else (row, other),
                device_id_type=MESH,
            ).start()
            return carry

        lax.fori_loop(1, count, send_sum, 0)
        pltpu.make_async_copy(
            buf.at[pl.ds(0, count - 1)], buf.at[pl.ds(0, count - 1)], sum_recv.at[r]
        ).wait()
        parts = [buf[i] for i in range(count)]
        while len(parts) > 1:
            pairs = [parts[i] + parts[i + 1] for i in range(0, len(parts) - 1, 2)]
            parts = pairs + ([parts[-1]] if len(parts) % 2 else [])
        total = parts[0]

    c0, c1, c2 = combination([total[i : i + 1] for i in range(6)])
    for t in range(2):
        out[t] = volt[t] + c0 * guess[t] + c1 * lifted[0][t] + c2 * lifted[1][t]

    for step in range(4):
        for way in range(4):
            halo_copy(step, way).wait_send()
    pltpu.make_async_copy(ask.at[everything], ask.at[everything], ask_send).wait()
    pltpu.make_async_copy(give.at[everything], give.at[everything], give_send).wait()
    for r, (axis, count, stride) in enumerate(rounds):
        part = reduce_bufs[r].at[pl.ds(0, count - 1)]
        pltpu.make_async_copy(part, part, sum_send.at[r]).wait()


def local(
    initial_voltage,
    inject,
    conduct,
    capacitance,
    track_gain,
    driver_tile,
    sink_net,
    sink_count,
    sink_tile,
    sink_node,
    sink_gain,
):
    n_row, n_col = lax.axis_size("row"), lax.axis_size("col")
    tiles, nodes, patterns = initial_voltage.shape[1:]
    edge = track_gain.shape[-1]
    slots = sink_net.shape[-1]
    rounds = ((0, n_row, 1), (1, 4, 1), (1, n_col // 4, 4))

    def by_slot(array):
        return jnp.swapaxes(array.reshape(n_col, slots), 0, 1)

    block = (tiles, nodes, patterns)
    vmem = pl.BlockSpec(memory_space=pltpu.VMEM)
    result = pl.pallas_call(
        functools.partial(kernel, (n_row, n_col, rounds)),
        out_shape=jax.ShapeDtypeStruct(block, F32),
        in_specs=[vmem] * 11,
        out_specs=vmem,
        scratch_shapes=[
            pltpu.VMEM((nodes, nodes), F32),
            pltpu.VMEM((nodes, nodes), F32),
            pltpu.VMEM((n_col * slots, patterns), F32),
            pltpu.VMEM((n_col * slots, patterns), F32),
            pltpu.VMEM((n_col * slots, patterns), F32),
            pltpu.VMEM((n_col * slots, patterns), F32),
            pltpu.VMEM((2 * edge + 8, patterns), F32),
            pltpu.VMEM((4, 2 * edge + 8, patterns), F32),
            pltpu.VMEM((3, 2, edge, patterns), F32),
            pltpu.VMEM((3, 4, 2, edge, patterns), F32),
            *[pltpu.VMEM((count, 8, patterns), F32) for _, count, _ in rounds],
            pltpu.SemaphoreType.DMA,
            pltpu.SemaphoreType.DMA,
            pltpu.SemaphoreType.DMA,
            pltpu.SemaphoreType.DMA,
            pltpu.SemaphoreType.DMA((4, 4)),
            pltpu.SemaphoreType.DMA((4, 4)),
            pltpu.SemaphoreType.DMA((len(rounds),)),
            pltpu.SemaphoreType.DMA((len(rounds),)),
        ],
        compiler_params=pltpu.CompilerParams(collective_id=0, has_side_effects=True),
        name="transient",
    )(
        initial_voltage.reshape(block),
        inject.reshape(block),
        conduct.reshape(block),
        capacitance.reshape(tiles, nodes),
        track_gain.reshape(2 * tiles, edge),
        driver_tile.reshape(1, -1),
        by_slot(sink_net),
        sink_count.reshape(1, n_col),
        by_slot(sink_tile),
        by_slot(sink_node),
        by_slot(sink_gain),
    )
    return result.reshape(initial_voltage.shape)


def solution(mesh):
    four = P("row", "col", None, None)
    three = P("row", "col", None)
    placed = (four, four, four, three, four, three, four, three, four, four, four)
    return jax.shard_map(local, mesh=mesh, in_specs=placed, out_specs=four, check_vma=False)
```

time: 709 us -> 59 us (0.08)
  blocking collectives: 498 us -> 0 us
  waiting for transfers between devices: 75.2 us -> 0 us
  starting transfers between devices: 57.1 us -> 0 us
  Pallas kernels: 0 us -> 57 us
  other arithmetic: 49.2 us -> 0 us
  between operations: 14.1 us -> 0.01 us
  local copies, waits for them, and re-layouts: 9.8 us -> 1.57 us
    psum x5 -> x0, blocking collectives: 498 us -> none  [the longest x3 294 us: residual_product(): return lax.psum(inner_sum(residual, precond), ('row', 'col'))]
    all_gather x1 -> x0, waiting for transfers between devices: 66.4 us -> none  [local(): gathered = lax.all_gather(drivers, 'col', axis=0, tiled=True)]
    ppermute x18 -> x0, starting transfers between devices: 57.1 us -> none  [the longest x8 27.8 us: padded_2(): lax.ppermute(lax.slice_in_dim(block, block.shape[dim] - width, None, axis...]
    pallas_call x0 -> x1, Pallas kernels: none -> 57 us  [local(): pl.pallas_call(functools.partial(kernel, (n_row, n_col, rounds)), out_sha...]
    another operation x7 -> x0, other arithmetic: 43.4 us -> none  [the longest x4 23.6 us: tile_inverse(): factors = jnp.linalg.cholesky(flat_blocks)]
    ppermute x18 -> x0, waiting for transfers between devices: 8.79 us -> none  [the longest x8 7.73 us: padded_2(): lax.ppermute(lax.slice_in_dim(block, block.shape[dim] - width, None, axis...]
  transfers between devices with their start and end apart: 19 -> 0, of which waited for: 11 -> 0; matrix products, arithmetic and copies ran while one was open for 1% -> 0% of each run, Pallas kernels for 0% -> 0%
where the time goes in v1:
time: 59 us; the launch traced here: 58.5 us
  Pallas kernels  57 us (97%)
  local copies, waits for them, and re-layouts  1.57 us (3%)
    pallas_call x1, Pallas kernels, local(): pl.pallas_call(functools.partial(kernel, (n_row, n_col, rounds)), out_sha...  57 us
    unnamed x1, local copies, waits for them, and re-layouts  1.57 us

profile of v1, /device:TPU:1, one launch (start us, length us, event | category | flops | bytes accessed | tf_op | source)
XLA Modules:
  0.0 58.5 jit_solution(12486200826034969804)
XLA Ops:
  0.0 57.0 %transient.1 = f32[2,128,128]{2,1,0:T(8,128)} custom-call(f32[2,128,128]{2,1,0:T(8,128)} %bitcast.21, f32[2,128,128]{2,1,0:T(8,128)} %bitcast.22, f32[2,128,128]{2,1,0:T(8,128)} %bitcast.23, f32[2,128]{1,0:T(2,128)} %bitcast.29, f32[4,32]{1,0:T(4,128)} %bitcast.28, s32[1,64]{1,0:T(1,128)} %bitcast.30, s32[8,32]{1,0:T(8,128)} %bitcast.24, s32[1,32]{1,0:T(1,128)} %bitcast.31, ...), custom_call_target="tpu_custom_call" | custom-call | tf_op jit(solution)/shard_map/transient/pallas_call | solution.py:418
  57.0 1.6 %copy.13 = f32[1,2,128,128]{3,2,1,0:T(8,128)} copy(f32[1,2,128,128]{3,2,1,0:T(8,128)} %bitcast.20) | data formatting | bytes 262144

commit v2 on v1

v2 whole, which is shorter than its diff:
```python
import functools

import jax
import jax.numpy as jnp
from jax import lax
from jax.experimental import pallas as pl
from jax.experimental.pallas import tpu as pltpu
from jax.sharding import PartitionSpec as P

F32 = jnp.float32
HIGH = lax.Precision.HIGHEST
MESH = pl.DeviceIdType.MESH
SCALE = 1.0 / 32.0
PIVOTS = 4
DEPTH = 3


def dot(left, right):
    return jnp.dot(left, right, precision=HIGH, preferred_element_type=F32)


def lane_splat(block, lane):
    return jnp.take_along_axis(block, jnp.full(block.shape, lane, jnp.int32), axis=1)


def pivot_rows(rows, first, offset, lane):
    mine = [rows[offset + i : offset + i + 1] for i in range(PIVOTS)]
    splats = [lane_splat(rows, first + j) for j in range(PIVOTS)]
    small = [
        [splats[j][offset + i : offset + i + 1] for j in range(PIVOTS)]
        for i in range(PIVOTS)
    ]
    for j in range(PIVOTS):
        scale = 1.0 / small[j][j]
        row = [scale if m == j else small[j][m] * scale for m in range(PIVOTS)]
        for i in range(PIVOTS):
            if i == j:
                continue
            factor = small[i][j]
            small[i] = [
                -factor * scale if m == j else small[i][m] - factor * row[m]
                for m in range(PIVOTS)
            ]
        small[j] = row
    fresh = []
    for i in range(PIVOTS):
        total = small[i][0] * mine[0]
        for j in range(1, PIVOTS):
            total = total + small[i][j] * mine[j]
        for j in range(PIVOTS):
            total = jnp.where(lane == first + j, small[i][j], total)
        fresh.append(total)
    return fresh


def eliminate(mats, start, stop):
    nodes = mats[0].shape[0]
    lane = lax.broadcasted_iota(jnp.int32, (1, nodes), 1)

    def group(index, carry):
        base = pl.multiple_of(index * 8, 8)
        for offset in range(0, 8, PIVOTS):
            first = base + offset
            whole = [mat[...] for mat in mats]
            rows = [mat[pl.ds(base, 8), :] for mat in mats]
            fresh = [pivot_rows(r, first, offset, lane) for r in rows]
            kept = (lane >= first) & (lane < first + PIVOTS)
            done = []
            for t in range(len(mats)):
                total = jnp.where(kept, 0.0, whole[t])
                for j in range(PIVOTS):
                    total = total - lane_splat(whole[t], first + j) * fresh[t][j]
                done.append(total)
            for t, mat in enumerate(mats):
                mat[...] = done[t]
                for j in range(PIVOTS):
                    mat[pl.ds(first + j, 1), :] = fresh[t][j]
        return carry

    lax.fori_loop(start, stop, group, 0)


def ring_peers(position, high_count, low_count):
    high, low = position // low_count, lax.rem(position, low_count)
    offsets = [(a, b) for a in range(high_count) for b in range(low_count) if a or b]
    offsets.sort(key=lambda o: -(min(o[0], high_count - o[0]) + min(o[1], low_count - o[1])))
    return [
        lax.rem(high + a, high_count) * low_count + lax.rem(low + b, low_count)
        for a, b in offsets
    ]


def near(depth):
    span = range(-depth - 1, depth + 3)
    return [
        (r, c) for r in span for c in span if abs(r) + max(-c, 0, c - 1) <= depth
    ]


def from_devices(tiles):
    held = {}
    for r, c in tiles:
        held.setdefault((r, c // 2), []).append(c % 2)
    held.pop((0, 0), None)
    far = lambda o: -(2 * abs(o[1]) + abs(o[0]))
    return {o: sorted(held[o]) for o in sorted(held, key=far)}


def gain_lines(depth):
    east, south = [], []
    for r, c in near(depth):
        east += [(r, c), (r, c - 1)]
        south += [(r, c), (r - 1, c)]
    return [(0, t) for t in dict.fromkeys(east)] + [(1, t) for t in dict.fromkeys(south)]


def column_sum(left, right):
    return jnp.sum(left * right, axis=0, keepdims=True)


def safe_inverse(value):
    return jnp.where(value > 0.0, 1.0 / value, 0.0)


def combination(n):
    up = 1.0 / SCALE
    h00, h01, h02 = n[0] + up * n[1], n[1] + up * n[2], n[2] + up * n[3]
    h11, h12, h22 = h02, n[3] + up * n[4], n[4] + up * n[5]
    inv0 = safe_inverse(h00)
    l10, l20 = h01 * inv0, h02 * inv0
    d11, d12, d22 = h11 - l10 * h01, h12 - l10 * h02, h22 - l20 * h02
    g1, g2 = n[1] - l10 * n[0], n[2] - l20 * n[0]
    inv1 = safe_inverse(d11)
    l21 = d12 * inv1
    c2 = (g2 - l21 * g1) * safe_inverse(d22 - l21 * d12)
    c1 = (g1 - d12 * c2) * inv1
    c0 = (n[0] - h01 * c1 - h02 * c2) * inv0
    return c0, c1, c2


def kernel(
    sizes,
    volt_hbm,
    inject_hbm,
    conduct_hbm,
    cap_hbm,
    track_hbm,
    driver_tile_hbm,
    sink_net_hbm,
    sink_count_hbm,
    sink_tile_hbm,
    sink_node_hbm,
    sink_gain_hbm,
    out,
    volt,
    inject,
    conduct,
    cap,
    track,
    driver_tile,
    sink_net,
    sink_count,
    sink_tile,
    sink_node,
    sink_gain,
    mat0,
    mat1,
    ask,
    asked,
    give,
    given,
    lines,
    lines_in,
    start_in,
    block_in,
    rims,
    rims_in,
    late,
    late_in,
    row_sums,
    col_sums,
    load_sem,
    ask_send,
    ask_recv,
    give_send,
    give_recv,
    lines_send,
    lines_recv,
    start_send,
    start_recv,
    block_send,
    block_recv,
    rims_send,
    rims_recv,
    late_send,
    late_recv,
    sum_send,
    sum_recv,
):
    n_row, n_col = sizes
    row, col = lax.axis_index("row"), lax.axis_index("col")
    nodes, edge = volt.shape[1], track.shape[1]
    slots = sink_net.shape[0]
    nets = driver_tile.shape[1]

    loads = [
        pltpu.make_async_copy(source, target, load_sem.at[i])
        for i, (source, target) in enumerate(
            (
                (sink_net_hbm, sink_net),
                (track_hbm, track),
                (volt_hbm, volt),
                (cap_hbm, cap),
                (conduct_hbm, conduct),
                (driver_tile_hbm, driver_tile),
                (sink_count_hbm, sink_count),
                (sink_tile_hbm, sink_tile),
                (sink_node_hbm, sink_node),
                (sink_gain_hbm, sink_gain),
                (inject_hbm, inject),
            )
        )
    ]
    for load in loads:
        load.start()

    row_group = [(position, col) for position in ring_peers(row, n_row // 2, 2)]
    col_group = [(row, position) for position in ring_peers(col, n_col // 4, 4)]
    wide = from_devices(near(DEPTH))
    blocks = from_devices(near(DEPTH - 1))
    tracks = from_devices([tile for _, tile in gain_lines(DEPTH - 1)])
    sides = from_devices(near(1))

    def device(offset):
        r, c = offset
        return (lax.rem(row + (n_row + r), n_row), lax.rem(col + (n_col + c), n_col))

    def back(offset):
        return device((-offset[0], -offset[1]))

    corners = [device(o) for o in wide if o[0] and o[1]]
    barrier = pltpu.get_barrier_semaphore()
    for peer in col_group + row_group + corners:
        pl.semaphore_signal(barrier, inc=1, device_id=peer, device_id_type=MESH)

    loads[0].wait()
    wanted = sink_net[...].astype(F32)
    for s in range(n_col):
        ask[s * slots : (s + 1) * slots, :] = jnp.broadcast_to(
            wanted[:, s : s + 1], (slots, nodes)
        )
    loads[1].wait()
    lines[...] = jnp.zeros(lines.shape, F32)
    lines[0:4, 0:edge] = track[...]
    loads[2].wait()

    pl.semaphore_wait(barrier, len(col_group) + len(row_group) + len(corners))

    def slot_rows(position):
        return pl.ds(pl.multiple_of(position * slots, slots), slots)

    def exchange(source, target, send, recv):
        for peer in col_group:
            pltpu.make_async_remote_copy(
                src_ref=source.at[slot_rows(peer[1])],
                dst_ref=target.at[slot_rows(col)],
                send_sem=send,
                recv_sem=recv,
                device_id=peer,
                device_id_type=MESH,
            ).start()

    def tile_part(ref, tiles):
        return ref if len(tiles) == 2 else ref.at[tiles[0]]

    def copies(sources, targets, users, send, recv):
        return [
            pltpu.make_async_remote_copy(
                src_ref=tile_part(sources, tiles),
                dst_ref=tile_part(targets.at[i], tiles),
                send_sem=send.at[i],
                recv_sem=recv.at[i],
                device_id=back(offset),
                device_id_type=MESH,
            )
            for i, (offset, tiles) in enumerate(users.items())
        ]

    exchange(ask, asked, ask_send, ask_recv)
    line_copies = [
        pltpu.make_async_remote_copy(
            src_ref=lines,
            dst_ref=lines_in.at[i],
            send_sem=lines_send.at[i],
            recv_sem=lines_recv.at[i],
            device_id=back(offset),
            device_id_type=MESH,
        )
        for i, offset in enumerate(tracks)
    ]
    start_copies = copies(volt.at[:, pl.ds(0, edge)], start_in, sides, start_send, start_recv)
    for copy in line_copies + start_copies:
        copy.start()
    asked[slot_rows(col), :] = ask[slot_rows(col), :]

    loads[3].wait()
    loads[4].wait()
    r_iota = lax.broadcasted_iota(jnp.int32, (nodes, nodes), 0)
    c_iota = lax.broadcasted_iota(jnp.int32, (nodes, nodes), 1)
    mats = (mat0, mat1)
    for t in range(2):
        mats[t][...] = conduct[t] + jnp.where(r_iota == c_iota, cap[t : t + 1, :], 0.0)
    groups = nodes // 8
    eliminate(mats, 0, groups // 2)

    loads[5].wait()
    lanes = lax.broadcasted_iota(jnp.int32, (1, 2 * nets), 1)
    tiles = jnp.concatenate([driver_tile[...], driver_tile[...]], axis=1)
    net_of = jnp.where(lanes >= nets, lanes - nets, lanes)
    tile_of = jnp.where(lanes >= nets, 1, 0)
    code = jnp.where(tiles == tile_of, net_of, -1).astype(F32)
    everything = pl.ds(0, (n_col - 1) * slots)
    pltpu.make_async_copy(asked.at[everything], asked.at[everything], ask_recv).wait()
    pick = jnp.where(asked[...] == code, 1.0, 0.0)
    give[...] = dot(pick, jnp.concatenate([volt[0, 0:nets, :], volt[1, 0:nets, :]], axis=0))
    exchange(give, given, give_send, give_recv)
    given[slot_rows(col), :] = give[slot_rows(col), :]

    eliminate(mats, groups // 2, groups)
    block_copies = []
    for i, (offset, held) in enumerate(blocks.items()):
        for t in held:
            block_copies.append(
                pltpu.make_async_remote_copy(
                    src_ref=mats[t].at[pl.ds(0, edge)],
                    dst_ref=block_in.at[i, t],
                    send_sem=block_send.at[i, t],
                    recv_sem=block_recv.at[i, t],
                    device_id=back(offset),
                    device_id_type=MESH,
                )
            )
    for copy in block_copies:
        copy.start()

    for load in loads[6:]:
        load.wait()
    slot_iota = lax.broadcasted_iota(jnp.int32, (slots, n_col), 0)
    weight = jnp.where(slot_iota < sink_count[...], sink_gain[...], 0.0)
    target = (sink_tile[...] * nodes + sink_node[...]).astype(F32)
    width = n_col * slots
    source = lax.broadcasted_iota(jnp.int32, (n_col, width), 0)
    place = lax.broadcasted_iota(jnp.int32, (n_col, width), 1)
    spread = jnp.where(place // slots == source, 1.0, 0.0)
    flat = dot(jnp.concatenate([target, weight], axis=0), spread)
    place = lax.broadcasted_iota(jnp.int32, (slots, width), 1)
    own = lax.rem(place, slots) == lax.broadcasted_iota(jnp.int32, (slots, width), 0)
    flat_target = jnp.sum(jnp.where(own, flat[:slots], 0.0), axis=0, keepdims=True)
    flat_weight = jnp.sum(jnp.where(own, flat[slots:], 0.0), axis=0, keepdims=True)
    node_row = lax.broadcasted_iota(jnp.int32, (2 * nodes, width), 0).astype(F32)
    scatter = jnp.where(node_row == flat_target, flat_weight, 0.0)

    base = [inject[t] - dot(conduct[t], volt[t]) for t in range(2)]

    def inside(offset):
        r, c = offset
        at_row, at_col = row + r, col + c
        return (at_row >= 0) & (at_row < n_row) & (at_col >= 0) & (at_col < n_col)

    present = {o: inside(o) for o in {**wide, **tracks}}

    def home(tile):
        return (tile[0], tile[1] // 2), tile[1] % 2

    def only_inside(tile, value):
        offset = home(tile)[0]
        return value if offset == (0, 0) else jnp.where(present[offset], value, 0.0)

    for copy in line_copies:
        copy.wait_recv()
    eye = lax.broadcasted_iota(jnp.int32, (edge, edge), 0) == lax.broadcasted_iota(
        jnp.int32, (edge, edge), 1
    )
    names = gain_lines(DEPTH - 1)
    place_of = {o: i for i, o in enumerate(tracks)}
    diagonals = []
    for way, tile in names:
        offset, t = home(tile)
        at = 2 * t + way
        if offset == (0, 0):
            line = track[at : at + 1, :]
        else:
            line = lines_in[place_of[offset], at : at + 1, 0:edge]
        diagonals.append(jnp.where(eye, only_inside(tile, line) * SCALE, 0.0))
    columns = dot(jnp.concatenate(diagonals, axis=0), jnp.ones((edge, nodes), F32))
    gains = {name: columns[i * edge : (i + 1) * edge] for i, name in enumerate(names)}

    def flow(tile, field):
        r, c = tile
        v = field[tile]
        total = gains[0, (r, c)] * (v - field[r, c + 1])
        total = total + gains[0, (r, c - 1)] * (v - field[r, c - 1])
        total = total + gains[1, (r, c)] * (v - field[r + 1, c])
        return total + gains[1, (r - 1, c)] * (v - field[r - 1, c])

    def gathered(depth, received, users, mine):
        field = {(0, t): mine[t] for t in range(2)}
        where = {o: i for i, o in enumerate(users)}
        for tile in near(depth):
            offset, t = home(tile)
            if offset != (0, 0):
                field[tile] = only_inside(tile, received[where[offset], t])
        return field

    own_tiles = ((0, 0), (0, 1))
    for copy in start_copies:
        copy.wait_recv()
    start = gathered(1, start_in, sides, [volt[t, 0:edge, :] for t in range(2)])
    first_flow = [flow(tile, start) for tile in own_tiles]
    pltpu.make_async_copy(given.at[everything], given.at[everything], give_recv).wait()
    current = dot(scatter, given[...])
    resid, guess = [], []
    for t in range(2):
        total = base[t] + current[t * nodes : (t + 1) * nodes]
        total = jnp.concatenate(
            [total[:edge] - first_flow[t] * (1.0 / SCALE), total[edge:]], axis=0
        )
        resid.append(total)
        guess.append(dot(mats[t][...], total))
        rims[t] = guess[t][:edge]

    rim_copies = copies(rims, rims_in, wide, rims_send, rims_recv)
    for copy in rim_copies:
        copy.start()
    moments = [sum(column_sum(guess[t], resid[t]) for t in range(2))]
    for copy in block_copies:
        copy.wait_recv()
    block = {(0, t): mats[t][0:edge, 0:edge] for t in range(2)}
    block_at = {o: i for i, o in enumerate(blocks)}
    for tile in near(DEPTH - 1):
        offset, t = home(tile)
        if offset != (0, 0):
            block[tile] = block_in[block_at[offset], t, :, 0:edge]
    for copy in rim_copies:
        copy.wait_recv()

    field = gathered(DEPTH, rims_in, wide, [guess[t][:edge] for t in range(2)])
    lifted, late_copies = [], []
    for step in range(3):
        reach = DEPTH - 1 - step
        if reach < 0:
            for t in range(2):
                late[t] = field[0, t]
            late_copies = copies(late, late_in, sides, late_send, late_recv)
            for copy in late_copies:
                copy.start()
            lifted.append([dot(mats[t][:, 0:edge], flows[0, t]) for t in range(2)])
            for copy in late_copies:
                copy.wait_recv()
            field = gathered(1, late_in, sides, [field[0, t] for t in range(2)])
            reach = 0
        flows = {tile: flow(tile, field) for tile in near(reach)}
        moments.append(sum(column_sum(field[0, t], flows[0, t]) for t in range(2)))
        if step < 2:
            if reach or DEPTH > 2:
                lifted.append([dot(mats[t][:, 0:edge], flows[0, t]) for t in range(2)])
            field = {
                tile: only_inside(tile, dot(block[tile], flows[tile])) for tile in near(reach)
            }
            moments.append(sum(column_sum(field[0, t], flows[0, t]) for t in range(2)))

    total = jnp.concatenate(moments + [jnp.zeros((2, nodes), F32)], axis=0)
    for r, (slot, group) in enumerate(((row, row_group), (col, col_group))):
        buf, count = (row_sums, col_sums)[r], len(group) + 1
        buf[slot] = total
        for peer in group:
            pltpu.make_async_remote_copy(
                src_ref=buf.at[slot],
                dst_ref=buf.at[slot],
                send_sem=sum_send.at[r],
                recv_sem=sum_recv.at[r],
                device_id=peer,
                device_id_type=MESH,
            ).start()
        part = buf.at[pl.ds(0, count - 1)]
        pltpu.make_async_copy(part, part, sum_recv.at[r]).wait()
        parts = [buf[i] for i in range(count)]
        while len(parts) > 1:
            pairs = [parts[i] + parts[i + 1] for i in range(0, len(parts) - 1, 2)]
            parts = pairs + ([parts[-1]] if len(parts) % 2 else [])
        total = parts[0]

    c0, c1, c2 = combination([total[i : i + 1] for i in range(6)])
    for t in range(2):
        out[t] = c0 * guess[t] + c1 * lifted[0][t] + c2 * lifted[1][t]

    for copy in line_copies + start_copies + block_copies + rim_copies + late_copies:
        copy.wait_send()
    pltpu.make_async_copy(ask.at[everything], ask.at[everything], ask_send).wait()
    pltpu.make_async_copy(give.at[everything], give.at[everything], give_send).wait()
    for r, group in enumerate((row_group, col_group)):
        part = (row_sums, col_sums)[r].at[pl.ds(0, len(group))]
        pltpu.make_async_copy(part, part, sum_send.at[r]).wait()


def local(
    initial_voltage,
    inject,
    conduct,
    capacitance,
    track_gain,
    driver_tile,
    sink_net,
    sink_count,
    sink_tile,
    sink_node,
    sink_gain,
):
    n_row, n_col = lax.axis_size("row"), lax.axis_size("col")
    tiles, nodes, patterns = initial_voltage.shape[1:]
    edge = track_gain.shape[-1]
    slots = sink_net.shape[-1]

    def by_slot(array):
        return jnp.swapaxes(array.reshape(n_col, slots), 0, 1)

    block = (tiles, nodes, patterns)
    arrays = (
        initial_voltage.reshape(block),
        inject.reshape(block),
        conduct.reshape(block),
        capacitance.reshape(tiles, nodes),
        track_gain.reshape(2 * tiles, edge),
        driver_tile.reshape(1, -1),
        by_slot(sink_net),
        sink_count.reshape(1, n_col),
        by_slot(sink_tile),
        by_slot(sink_node),
        by_slot(sink_gain),
    )
    rim = (tiles, edge, patterns)
    wide, blocks = from_devices(near(DEPTH)), from_devices(near(DEPTH - 1))
    tracks = from_devices([tile for _, tile in gain_lines(DEPTH - 1)])
    dma = pltpu.SemaphoreType.DMA
    slot_rows = pltpu.VMEM((n_col * slots, patterns), F32)
    result = pl.pallas_call(
        functools.partial(kernel, (n_row, n_col)),
        out_shape=jax.ShapeDtypeStruct(block, F32),
        in_specs=[pl.BlockSpec(memory_space=pltpu.HBM)] * len(arrays),
        out_specs=pl.BlockSpec(memory_space=pltpu.VMEM),
        scratch_shapes=[
            *[pltpu.VMEM(array.shape, array.dtype) for array in arrays],
            pltpu.VMEM((nodes, nodes), F32),
            pltpu.VMEM((nodes, nodes), F32),
            *[slot_rows] * 4,
            pltpu.VMEM((8, patterns), F32),
            pltpu.VMEM((len(tracks), 8, patterns), F32),
            pltpu.VMEM((4, *rim), F32),
            pltpu.VMEM((len(blocks), *rim), F32),
            pltpu.VMEM(rim, F32),
            pltpu.VMEM((len(wide), *rim), F32),
            pltpu.VMEM(rim, F32),
            pltpu.VMEM((4, *rim), F32),
            pltpu.VMEM((n_row, 8, patterns), F32),
            pltpu.VMEM((n_col, 8, patterns), F32),
            dma((len(arrays),)),
            *[dma] * 4,
            *[dma((len(tracks),))] * 2,
            *[dma((4,))] * 2,
            *[dma((len(blocks), tiles))] * 2,
            *[dma((len(wide),))] * 2,
            *[dma((4,))] * 2,
            *[dma((2,))] * 2,
        ],
        compiler_params=pltpu.CompilerParams(
            collective_id=0, has_side_effects=True
        ),
        name="transient",
    )(*arrays)
    return initial_voltage + result.reshape(initial_voltage.shape)


def solution(mesh):
    four = P("row", "col", None, None)
    three = P("row", "col", None)
    placed = (four, four, four, three, four, three, four, three, four, four, four)
    return jax.shard_map(local, mesh=mesh, in_specs=placed, out_specs=four, check_vma=False)
```

time: 59 us -> 50.8 us (0.86)
  Pallas kernels: 57 us -> 49 us
  other arithmetic: 0 us -> 1.57 us
  local copies, waits for them, and re-layouts: 1.57 us -> 0.01 us
    pallas_call x1, Pallas kernels: 57 us -> 49 us  [local(): pl.pallas_call(functools.partial(kernel, (n_row, n_col)), out_shape=jax.S...]
    add x0 -> x1, other arithmetic: none -> 1.57 us  [local(): return initial_voltage + result.reshape(initial_voltage.shape)]
    unnamed x1 -> x2, local copies, waits for them, and re-layouts: 1.57 us -> 0.01 us
where the time goes in v2:
time: 50.8 us; the launch traced here: 50.6 us
  Pallas kernels  49 us (96%)
  other arithmetic  1.57 us (3%)
    pallas_call x1, Pallas kernels, local(): pl.pallas_call(functools.partial(kernel, (n_row, n_col)), out_shape=jax.S...  49 us
    add x1, other arithmetic, local(): return initial_voltage + result.reshape(initial_voltage.shape)  1.57 us

profile of v2, /device:TPU:1, one launch (start us, length us, event | category | flops | bytes accessed | tf_op | source)
XLA Modules:
  0.0 50.6 jit_solution(13634295977504205781)
XLA Ops:
  0.0 0.0 copy-start
  0.0 49.0 %transient.1 = f32[2,128,128]{2,1,0:T(8,128)} custom-call(f32[2,128,128]{2,1,0:T(8,128)} %bitcast.21, f32[2,128,128]{2,1,0:T(8,128)} %bitcast.22, f32[2,128,128]{2,1,0:T(8,128)} %bitcast.23, f32[2,128]{1,0:T(2,128)} %bitcast.29, f32[4,32]{1,0:T(4,128)} %bitcast.28, s32[1,64]{1,0:T(1,128)} %bitcast.30, s32[8,32]{1,0:T(8,128)} %bitcast.24, s32[1,32]{1,0:T(1,128)} %bitcast.31, ...), custom_call_target="tpu_custom_call" | custom-call | tf_op jit(solution)/shard_map/transient/pallas_call | solution.py:546
  49.0 0.0 copy-done
  49.0 1.6 %bitcast_add_fusion = f32[1,2,128,128]{3,2,1,0:T(8,128)} fusion(f32[1,2,128,128]{3,2,1,0:T(8,128)S(1)} %copy-done, f32[2,128,128]{2,1,0:T(8,128)} %transient.1), kind=kLoop, calls=%fused_computation | loop fusion | flops 32768 | bytes 393216 | tf_op jit(solution)/shard_map/add | solution.py:580
Async XLA Ops:
  0.0 49.0 %copy-start = (f32[1,2,128,128]{3,2,1,0:T(8,128)S(1)}, f32[1,2,128,128]{3,2,1,0:T(8,128)}, u32[]{:S(2)}) copy-start(f32[1,2,128,128]{3,2,1,0:T(8,128)} %param.11) | copy-start | bytes 393220

commit v3 on v2

--- a/solution.py
+++ b/solution.py
@@ -417,22 +417,33 @@
         copy.wait_recv()
     start = gathered(1, start_in, sides, [volt[t, 0:edge, :] for t in range(2)])
     first_flow = [flow(tile, start) for tile in own_tiles]
+    calm = []
+    for t in range(2):
+        calm.append(
+            jnp.concatenate(
+                [base[t][:edge] - first_flow[t] * (1.0 / SCALE), base[t][edge:]], axis=0
+            )
+        )
+    calm_rim = [dot(mats[t][0:edge, :], calm[t]) for t in range(2)]
+    spread_rim = jnp.concatenate(
+        [dot(mats[t][0:edge, :], scatter[t * nodes : (t + 1) * nodes]) for t in range(2)], axis=0
+    )
     pltpu.make_async_copy(given.at[everything], given.at[everything], give_recv).wait()
-    current = dot(scatter, given[...])
-    resid, guess = [], []
+    lift = dot(spread_rim, given[...])
+    own_rim = [calm_rim[t] + lift[t * edge : (t + 1) * edge] for t in range(2)]
     for t in range(2):
-        total = base[t] + current[t * nodes : (t + 1) * nodes]
-        total = jnp.concatenate(
-            [total[:edge] - first_flow[t] * (1.0 / SCALE), total[edge:]], axis=0
-        )
-        resid.append(total)
-        guess.append(dot(mats[t][...], total))
-        rims[t] = guess[t][:edge]
-
+        rims[t] = own_rim[t]
     rim_copies = copies(rims, rims_in, wide, rims_send, rims_recv)
     for copy in rim_copies:
         copy.start()
-    moments = [sum(column_sum(guess[t], resid[t]) for t in range(2))]
+    current = dot(scatter, given[...])
+    guess = []
+    for t in range(2):
+        resid = calm[t] + current[t * nodes : (t + 1) * nodes]
+        rest = dot(mats[t][edge:, :], resid)
+        guess.append(jnp.concatenate([own_rim[t], rest], axis=0))
+        part = column_sum(guess[t], resid)
+        moments = [part if t == 0 else moments[0] + part]
     for copy in block_copies:
         copy.wait_recv()
     block = {(0, t): mats[t][0:edge, 0:edge] for t in range(2)}
@@ -444,7 +455,7 @@
     for copy in rim_copies:
         copy.wait_recv()
 
-    field = gathered(DEPTH, rims_in, wide, [guess[t][:edge] for t in range(2)])
+    field = gathered(DEPTH, rims_in, wide, own_rim)
     lifted, late_copies = [], []
     for step in range(3):
         reach = DEPTH - 1 - step
@@ -545,7 +556,7 @@
     slot_rows = pltpu.VMEM((n_col * slots, patterns), F32)
     result = pl.pallas_call(
         functools.partial(kernel, (n_row, n_col)),
-        out_shape=jax.ShapeDtypeStruct(block, F32),
+        out_shape=pltpu.VMEM(block, F32),
         in_specs=[pl.BlockSpec(memory_space=pltpu.HBM)] * len(arrays),
         out_specs=pl.BlockSpec(memory_space=pltpu.VMEM),
         scratch_shapes=[

time: 50.8 us -> 48.6 us (0.957)
  Pallas kernels: 49 us -> 47.7 us
  other arithmetic: 1.57 us -> 0.67 us
    pallas_call x1, Pallas kernels: 49 us -> 47.7 us  [local(): pl.pallas_call(functools.partial(kernel, (n_row, n_col)), out_shape=pltpu...]
    add x1, other arithmetic: 1.57 us -> 0.67 us  [local(): return initial_voltage + result.reshape(initial_voltage.shape)]
where the time goes in v3:
time: 48.6 us; the launch traced here: 48.4 us
  Pallas kernels  47.7 us (98%)
  other arithmetic  0.67 us (1%)
    pallas_call x1, Pallas kernels, local(): pl.pallas_call(functools.partial(kernel, (n_row, n_col)), out_shape=pltpu...  47.7 us

profile of v3, /device:TPU:1, one launch (start us, length us, event | category | flops | bytes accessed | tf_op | source)
XLA Modules:
  0.0 48.4 jit_solution(8608946767278838331)
XLA Ops:
  0.0 0.0 copy-start
  0.0 47.7 %transient.1 = f32[2,128,128]{2,1,0:T(8,128)S(1)} custom-call(f32[2,128,128]{2,1,0:T(8,128)} %bitcast.21, f32[2,128,128]{2,1,0:T(8,128)} %bitcast.22, f32[2,128,128]{2,1,0:T(8,128)} %bitcast.23, f32[2,128]{1,0:T(2,128)} %bitcast.29, f32[4,32]{1,0:T(4,128)} %bitcast.28, s32[1,64]{1,0:T(1,128)} %bitcast.30, s32[8,32]{1,0:T(8,128)} %bitcast.24, ...), custom_call_target="tpu_custom_call" | custom-call | tf_op jit(solution)/shard_map/transient/pallas_call | solution.py:557
  47.8 0.0 copy-done
  47.8 0.7 %bitcast_add_fusion = f32[1,2,128,128]{3,2,1,0:T(8,128)} fusion(f32[1,2,128,128]{3,2,1,0:T(8,128)S(1)} %copy-done, f32[2,128,128]{2,1,0:T(8,128)S(1)} %transient.1), kind=kLoop, calls=%fused_computation | loop fusion | flops 32768 | bytes 393216 | tf_op jit(solution)/shard_map/add | solution.py:591
Async XLA Ops:
  0.0 47.8 %copy-start = (f32[1,2,128,128]{3,2,1,0:T(8,128)S(1)}, f32[1,2,128,128]{3,2,1,0:T(8,128)}, u32[]{:S(2)}) copy-start(f32[1,2,128,128]{3,2,1,0:T(8,128)} %param.11) | copy-start | bytes 393220

commit v4 on v3

--- a/solution.py
+++ b/solution.py
@@ -17,6 +17,21 @@
 
 def dot(left, right):
     return jnp.dot(left, right, precision=HIGH, preferred_element_type=F32)
+
+
+def thirds(values):
+    parts = []
+    for _ in range(3):
+        part = values.astype(jnp.bfloat16)
+        parts.append(part)
+        values = values - part.astype(F32)
+    return parts
+
+
+def dot_thirds(left, right):
+    pairs = [(p, right) for p in left] if isinstance(left, list) else [(left, p) for p in right]
+    first, second, third = (jnp.dot(a, b, preferred_element_type=F32) for a, b in pairs)
+    return first + (second + third)
 
 
 def lane_splat(block, lane):
@@ -203,6 +218,25 @@
     slots = sink_net.shape[0]
     nets = driver_tile.shape[1]
 
+    row_group = [(position, col) for position in ring_peers(row, n_row // 2, 2)]
+    col_group = [(row, position) for position in ring_peers(col, n_col // 4, 4)]
+    wide = from_devices(near(DEPTH))
+    blocks = from_devices(near(DEPTH - 1))
+    tracks = from_devices([tile for _, tile in gain_lines(DEPTH - 1)])
+    sides = from_devices(near(1))
+
+    def device(offset):
+        r, c = offset
+        return (lax.rem(row + (n_row + r), n_row), lax.rem(col + (n_col + c), n_col))
+
+    def back(offset):
+        return device((-offset[0], -offset[1]))
+
+    corners = [device(o) for o in wide if o[0] and o[1]]
+    barrier = pltpu.get_barrier_semaphore()
+    for peer in col_group + row_group + corners:
+        pl.semaphore_signal(barrier, inc=1, device_id=peer, device_id_type=MESH)
+
     loads = [
         pltpu.make_async_copy(source, target, load_sem.at[i])
         for i, (source, target) in enumerate(
@@ -224,25 +258,6 @@
     for load in loads:
         load.start()
 
-    row_group = [(position, col) for position in ring_peers(row, n_row // 2, 2)]
-    col_group = [(row, position) for position in ring_peers(col, n_col // 4, 4)]
-    wide = from_devices(near(DEPTH))
-    blocks = from_devices(near(DEPTH - 1))
-    tracks = from_devices([tile for _, tile in gain_lines(DEPTH - 1)])
-    sides = from_devices(near(1))
-
-    def device(offset):
-        r, c = offset
-        return (lax.rem(row + (n_row + r), n_row), lax.rem(col + (n_col + c), n_col))
-
-    def back(offset):
-        return device((-offset[0], -offset[1]))
-
-    corners = [device(o) for o in wide if o[0] and o[1]]
-    barrier = pltpu.get_barrier_semaphore()
-    for peer in col_group + row_group + corners:
-        pl.semaphore_signal(barrier, inc=1, device_id=peer, device_id_type=MESH)
-
     loads[0].wait()
     wanted = sink_net[...].astype(F32)
     for s in range(n_col):
@@ -253,6 +268,33 @@
     lines[...] = jnp.zeros(lines.shape, F32)
     lines[0:4, 0:edge] = track[...]
     loads[2].wait()
+
+    for load in loads[3:]:
+        load.wait()
+    slot_iota = lax.broadcasted_iota(jnp.int32, (slots, n_col), 0)
+    weight = jnp.where(slot_iota < sink_count[...], sink_gain[...], 0.0)
+    target = (sink_tile[...] * nodes + sink_node[...]).astype(F32)
+    width = n_col * slots
+    source = lax.broadcasted_iota(jnp.int32, (n_col, width), 0)
+    place = lax.broadcasted_iota(jnp.int32, (n_col, width), 1)
+    spread = jnp.where(place // slots == source, 1.0, 0.0)
+    flat = dot(jnp.concatenate([target, weight], axis=0), spread)
+    place = lax.broadcasted_iota(jnp.int32, (slots, width), 1)
+    own = lax.rem(place, slots) == lax.broadcasted_iota(jnp.int32, (slots, width), 0)
+    flat_target = jnp.sum(jnp.where(own, flat[:slots], 0.0), axis=0, keepdims=True)
+    flat_weight = jnp.sum(jnp.where(own, flat[slots:], 0.0), axis=0, keepdims=True)
+    node_row = lax.broadcasted_iota(jnp.int32, (2 * nodes, width), 0).astype(F32)
+    scatter = jnp.where(node_row == flat_target, flat_weight, 0.0)
+
+    base = [inject[t] - dot(conduct[t], volt[t]) for t in range(2)]
+
+    lanes = lax.broadcasted_iota(jnp.int32, (1, 2 * nets), 1)
+    tiles = jnp.concatenate([driver_tile[...], driver_tile[...]], axis=1)
+    net_of = jnp.where(lanes >= nets, lanes - nets, lanes)
+    tile_of = jnp.where(lanes >= nets, 1, 0)
+    code = jnp.where(tiles == tile_of, net_of, -1).astype(F32)
+    driver_rows = thirds(jnp.concatenate([volt[0, 0:nets, :], volt[1, 0:nets, :]], axis=0))
+
 
     pl.semaphore_wait(barrier, len(col_group) + len(row_group) + len(corners))
 
@@ -303,8 +345,6 @@
         copy.start()
     asked[slot_rows(col), :] = ask[slot_rows(col), :]
 
-    loads[3].wait()
-    loads[4].wait()
     r_iota = lax.broadcasted_iota(jnp.int32, (nodes, nodes), 0)
     c_iota = lax.broadcasted_iota(jnp.int32, (nodes, nodes), 1)
     mats = (mat0, mat1)
@@ -313,16 +353,10 @@
     groups = nodes // 8
     eliminate(mats, 0, groups // 2)
 
-    loads[5].wait()
-    lanes = lax.broadcasted_iota(jnp.int32, (1, 2 * nets), 1)
-    tiles = jnp.concatenate([driver_tile[...], driver_tile[...]], axis=1)
-    net_of = jnp.where(lanes >= nets, lanes - nets, lanes)
-    tile_of = jnp.where(lanes >= nets, 1, 0)
-    code = jnp.where(tiles == tile_of, net_of, -1).astype(F32)
     everything = pl.ds(0, (n_col - 1) * slots)
     pltpu.make_async_copy(asked.at[everything], asked.at[everything], ask_recv).wait()
-    pick = jnp.where(asked[...] == code, 1.0, 0.0)
-    give[...] = dot(pick, jnp.concatenate([volt[0, 0:nets, :], volt[1, 0:nets, :]], axis=0))
+    pick = jnp.where(asked[...] == code, 1.0, 0.0).astype(jnp.bfloat16)
+    give[...] = dot_thirds(pick, driver_rows)
     exchange(give, given, give_send, give_recv)
     given[slot_rows(col), :] = give[slot_rows(col), :]
 
@@ -343,25 +377,6 @@
     for copy in block_copies:
         copy.start()
 
-    for load in loads[6:]:
-        load.wait()
-    slot_iota = lax.broadcasted_iota(jnp.int32, (slots, n_col), 0)
-    weight = jnp.where(slot_iota < sink_count[...], sink_gain[...], 0.0)
-    target = (sink_tile[...] * nodes + sink_node[...]).astype(F32)
-    width = n_col * slots
-    source = lax.broadcasted_iota(jnp.int32, (n_col, width), 0)
-    place = lax.broadcasted_iota(jnp.int32, (n_col, width), 1)
-    spread = jnp.where(place // slots == source, 1.0, 0.0)
-    flat = dot(jnp.concatenate([target, weight], axis=0), spread)
-    place = lax.broadcasted_iota(jnp.int32, (slots, width), 1)
-    own = lax.rem(place, slots) == lax.broadcasted_iota(jnp.int32, (slots, width), 0)
-    flat_target = jnp.sum(jnp.where(own, flat[:slots], 0.0), axis=0, keepdims=True)
-    flat_weight = jnp.sum(jnp.where(own, flat[slots:], 0.0), axis=0, keepdims=True)
-    node_row = lax.broadcasted_iota(jnp.int32, (2 * nodes, width), 0).astype(F32)
-    scatter = jnp.where(node_row == flat_target, flat_weight, 0.0)
-
-    base = [inject[t] - dot(conduct[t], volt[t]) for t in range(2)]
-
     def inside(offset):
         r, c = offset
         at_row, at_col = row + r, col + c
@@ -392,7 +407,9 @@
         else:
             line = lines_in[place_of[offset], at : at + 1, 0:edge]
         diagonals.append(jnp.where(eye, only_inside(tile, line) * SCALE, 0.0))
-    columns = dot(jnp.concatenate(diagonals, axis=0), jnp.ones((edge, nodes), F32))
+    columns = dot_thirds(
+        thirds(jnp.concatenate(diagonals, axis=0)), jnp.ones((edge, nodes), jnp.bfloat16)
+    )
     gains = {name: columns[i * edge : (i + 1) * edge] for i, name in enumerate(names)}
 
     def flow(tile, field):
@@ -480,22 +497,23 @@
             }
             moments.append(sum(column_sum(field[0, t], flows[0, t]) for t in range(2)))
 
-    total = jnp.concatenate(moments + [jnp.zeros((2, nodes), F32)], axis=0)
+    total = jnp.concatenate(moments, axis=0)
+    used = pl.ds(0, len(moments))
     for r, (slot, group) in enumerate(((row, row_group), (col, col_group))):
         buf, count = (row_sums, col_sums)[r], len(group) + 1
-        buf[slot] = total
+        buf[slot, used] = total
         for peer in group:
             pltpu.make_async_remote_copy(
-                src_ref=buf.at[slot],
-                dst_ref=buf.at[slot],
+                src_ref=buf.at[slot, used],
+                dst_ref=buf.at[slot, used],
                 send_sem=sum_send.at[r],
                 recv_sem=sum_recv.at[r],
                 device_id=peer,
                 device_id_type=MESH,
             ).start()
-        part = buf.at[pl.ds(0, count - 1)]
+        part = buf.at[pl.ds(0, count - 1), used]
         pltpu.make_async_copy(part, part, sum_recv.at[r]).wait()
-        parts = [buf[i] for i in range(count)]
+        parts = [buf[i, used] for i in range(count)]
         while len(parts) > 1:
             pairs = [parts[i] + parts[i + 1] for i in range(0, len(parts) - 1, 2)]
             parts = pairs + ([parts[-1]] if len(parts) % 2 else [])
@@ -510,7 +528,7 @@
     pltpu.make_async_copy(ask.at[everything], ask.at[everything], ask_send).wait()
     pltpu.make_async_copy(give.at[everything], give.at[everything], give_send).wait()
     for r, group in enumerate((row_group, col_group)):
-        part = (row_sums, col_sums)[r].at[pl.ds(0, len(group))]
+        part = (row_sums, col_sums)[r].at[pl.ds(0, len(group)), used]
         pltpu.make_async_copy(part, part, sum_send.at[r]).wait()
 
 

time: 48.6 us -> 47.6 us (0.979)
  Pallas kernels: 47.7 us -> 46.8 us
    pallas_call x1, Pallas kernels: 47.7 us -> 46.8 us  [local(): pl.pallas_call(functools.partial(kernel, (n_row, n_col)), out_shape=pltpu...]
where the time goes in v4:
time: 47.6 us; the launch traced here: 47.4 us
  Pallas kernels  46.8 us (98%)
  other arithmetic  0.67 us (1%)
    pallas_call x1, Pallas kernels, local(): pl.pallas_call(functools.partial(kernel, (n_row, n_col)), out_shape=pltpu...  46.8 us

profile of v4, /device:TPU:1, one launch (start us, length us, event | category | flops | bytes accessed | tf_op | source)
XLA Modules:
  0.0 47.4 jit_solution(11156889176751244227)
XLA Ops:
  0.0 0.0 copy-start
  0.0 46.8 %transient.1 = f32[2,128,128]{2,1,0:T(8,128)S(1)} custom-call(f32[2,128,128]{2,1,0:T(8,128)} %bitcast.21, f32[2,128,128]{2,1,0:T(8,128)} %bitcast.22, f32[2,128,128]{2,1,0:T(8,128)} %bitcast.23, f32[2,128]{1,0:T(2,128)} %bitcast.29, f32[4,32]{1,0:T(4,128)} %bitcast.28, s32[1,64]{1,0:T(1,128)} %bitcast.30, s32[8,32]{1,0:T(8,128)} %bitcast.24, ...), custom_call_target="tpu_custom_call" | custom-call | tf_op jit(solution)/shard_map/transient/pallas_call | solution.py:575
  46.8 0.0 copy-done
  46.8 0.7 %bitcast_add_fusion = f32[1,2,128,128]{3,2,1,0:T(8,128)} fusion(f32[1,2,128,128]{3,2,1,0:T(8,128)S(1)} %copy-done, f32[2,128,128]{2,1,0:T(8,128)S(1)} %transient.1), kind=kLoop, calls=%fused_computation | loop fusion | flops 32768 | bytes 393216 | tf_op jit(solution)/shard_map/add | solution.py:609
Async XLA Ops:
  0.0 46.8 %copy-start = (f32[1,2,128,128]{3,2,1,0:T(8,128)S(1)}, f32[1,2,128,128]{3,2,1,0:T(8,128)}, u32[]{:S(2)}) copy-start(f32[1,2,128,128]{3,2,1,0:T(8,128)} %param.11) | copy-start | bytes 393220

commit v5 on v4

--- a/solution.py
+++ b/solution.py
@@ -259,11 +259,16 @@
         load.start()
 
     loads[0].wait()
-    wanted = sink_net[...].astype(F32)
-    for s in range(n_col):
-        ask[s * slots : (s + 1) * slots, :] = jnp.broadcast_to(
-            wanted[:, s : s + 1], (slots, nodes)
-        )
+    wanted = sink_net[...].astype(jnp.bfloat16)
+    to_lane = jnp.where(
+        lax.broadcasted_iota(jnp.int32, (slots, nodes), 0)
+        == lax.broadcasted_iota(jnp.int32, (slots, nodes), 1),
+        1.0,
+        0.0,
+    ).astype(jnp.bfloat16)
+    ask[pl.ds(0, n_col, stride=slots), :] = lax.dot_general(
+        wanted, to_lane, (((0,), (0,)), ((), ())), preferred_element_type=F32
+    )
     loads[1].wait()
     lines[...] = jnp.zeros(lines.shape, F32)
     lines[0:4, 0:edge] = track[...]
@@ -298,14 +303,14 @@
 
     pl.semaphore_wait(barrier, len(col_group) + len(row_group) + len(corners))
 
-    def slot_rows(position):
-        return pl.ds(pl.multiple_of(position * slots, slots), slots)
-
-    def exchange(source, target, send, recv):
+    def slot_rows(position, count=slots):
+        return pl.ds(pl.multiple_of(position * slots, slots), count)
+
+    def exchange(source, target, send, recv, count=slots):
         for peer in col_group:
             pltpu.make_async_remote_copy(
-                src_ref=source.at[slot_rows(peer[1])],
-                dst_ref=target.at[slot_rows(col)],
+                src_ref=source.at[slot_rows(peer[1], count)],
+                dst_ref=target.at[slot_rows(col, count)],
                 send_sem=send,
                 recv_sem=recv,
                 device_id=peer,
@@ -328,7 +333,7 @@
             for i, (offset, tiles) in enumerate(users.items())
         ]
 
-    exchange(ask, asked, ask_send, ask_recv)
+    exchange(ask, asked, ask_send, ask_recv, 1)
     line_copies = [
         pltpu.make_async_remote_copy(
             src_ref=lines,
@@ -343,7 +348,7 @@
     start_copies = copies(volt.at[:, pl.ds(0, edge)], start_in, sides, start_send, start_recv)
     for copy in line_copies + start_copies:
         copy.start()
-    asked[slot_rows(col), :] = ask[slot_rows(col), :]
+    asked[slot_rows(col, 1), :] = ask[slot_rows(col, 1), :]
 
     r_iota = lax.broadcasted_iota(jnp.int32, (nodes, nodes), 0)
     c_iota = lax.broadcasted_iota(jnp.int32, (nodes, nodes), 1)
@@ -353,10 +358,19 @@
     groups = nodes // 8
     eliminate(mats, 0, groups // 2)
 
-    everything = pl.ds(0, (n_col - 1) * slots)
-    pltpu.make_async_copy(asked.at[everything], asked.at[everything], ask_recv).wait()
-    pick = jnp.where(asked[...] == code, 1.0, 0.0).astype(jnp.bfloat16)
-    give[...] = dot_thirds(pick, driver_rows)
+    everything, each = pl.ds(0, (n_col - 1) * slots), pl.ds(0, n_col - 1)
+    pltpu.make_async_copy(asked.at[each], asked.at[each], ask_recv).wait()
+    wish = asked[pl.ds(0, n_col, stride=slots), :]
+    pick = jnp.concatenate(
+        [
+            jnp.where(jnp.broadcast_to(wish[:, k : k + 1], (n_col, 2 * nets)) == code, 1.0, 0.0)
+            for k in range(slots)
+        ],
+        axis=0,
+    ).astype(jnp.bfloat16)
+    answer = dot_thirds(pick, driver_rows)
+    for k in range(slots):
+        give[pl.ds(k, n_col, stride=slots), :] = answer[k * n_col : (k + 1) * n_col]
     exchange(give, given, give_send, give_recv)
     given[slot_rows(col), :] = give[slot_rows(col), :]
 
@@ -525,7 +539,7 @@
 
     for copy in line_copies + start_copies + block_copies + rim_copies + late_copies:
         copy.wait_send()
-    pltpu.make_async_copy(ask.at[everything], ask.at[everything], ask_send).wait()
+    pltpu.make_async_copy(ask.at[each], ask.at[each], ask_send).wait()
     pltpu.make_async_copy(give.at[everything], give.at[everything], give_send).wait()
     for r, group in enumerate((row_group, col_group)):
         part = (row_sums, col_sums)[r].at[pl.ds(0, len(group)), used]

time: 47.6 us -> 47.1 us (0.989)
  Pallas kernels: 46.8 us -> 46.3 us
    pallas_call x1, Pallas kernels: 46.8 us -> 46.3 us  [local(): pl.pallas_call(functools.partial(kernel, (n_row, n_col)), out_shape=pltpu...]
where the time goes in v5:
time: 47.1 us; the launch traced here: 47 us
  Pallas kernels  46.3 us (98%)
  other arithmetic  0.67 us (1%)
    pallas_call x1, Pallas kernels, local(): pl.pallas_call(functools.partial(kernel, (n_row, n_col)), out_shape=pltpu...  46.3 us

profile of v5, /device:TPU:1, one launch (start us, length us, event | category | flops | bytes accessed | tf_op | source)
XLA Modules:
  0.0 47.0 jit_solution(16825259040811102816)
XLA Ops:
  0.0 0.0 copy-start
  0.0 46.3 %transient.1 = f32[2,128,128]{2,1,0:T(8,128)S(1)} custom-call(f32[2,128,128]{2,1,0:T(8,128)} %bitcast.21, f32[2,128,128]{2,1,0:T(8,128)} %bitcast.22, f32[2,128,128]{2,1,0:T(8,128)} %bitcast.23, f32[2,128]{1,0:T(2,128)} %bitcast.29, f32[4,32]{1,0:T(4,128)} %bitcast.28, s32[1,64]{1,0:T(1,128)} %bitcast.30, s32[8,32]{1,0:T(8,128)} %bitcast.24, ...), custom_call_target="tpu_custom_call" | custom-call | tf_op jit(solution)/shard_map/transient/pallas_call | solution.py:589
  46.3 0.0 copy-done
  46.3 0.7 %bitcast_add_fusion = f32[1,2,128,128]{3,2,1,0:T(8,128)} fusion(f32[1,2,128,128]{3,2,1,0:T(8,128)S(1)} %copy-done, f32[2,128,128]{2,1,0:T(8,128)S(1)} %transient.1), kind=kLoop, calls=%fused_computation | loop fusion | flops 32768 | bytes 393216 | tf_op jit(solution)/shard_map/add | solution.py:623
Async XLA Ops:
  0.0 46.3 %copy-start = (f32[1,2,128,128]{3,2,1,0:T(8,128)S(1)}, f32[1,2,128,128]{3,2,1,0:T(8,128)}, u32[]{:S(2)}) copy-start(f32[1,2,128,128]{3,2,1,0:T(8,128)} %param.11) | copy-start | bytes 393220

commit v6 on v5

--- a/solution.py
+++ b/solution.py
@@ -487,7 +487,7 @@
         copy.wait_recv()
 
     field = gathered(DEPTH, rims_in, wide, own_rim)
-    lifted, late_copies = [], []
+    pushed, late_copies = [], []
     for step in range(3):
         reach = DEPTH - 1 - step
         if reach < 0:
@@ -496,7 +496,6 @@
             late_copies = copies(late, late_in, sides, late_send, late_recv)
             for copy in late_copies:
                 copy.start()
-            lifted.append([dot(mats[t][:, 0:edge], flows[0, t]) for t in range(2)])
             for copy in late_copies:
                 copy.wait_recv()
             field = gathered(1, late_in, sides, [field[0, t] for t in range(2)])
@@ -504,8 +503,7 @@
         flows = {tile: flow(tile, field) for tile in near(reach)}
         moments.append(sum(column_sum(field[0, t], flows[0, t]) for t in range(2)))
         if step < 2:
-            if reach or DEPTH > 2:
-                lifted.append([dot(mats[t][:, 0:edge], flows[0, t]) for t in range(2)])
+            pushed.append([flows[0, t] for t in range(2)])
             field = {
                 tile: only_inside(tile, dot(block[tile], flows[tile])) for tile in near(reach)
             }
@@ -525,6 +523,8 @@
                 device_id=peer,
                 device_id_type=MESH,
             ).start()
+        if r == 0:
+            lifted = [[dot(mats[t][:, 0:edge], step[t]) for t in range(2)] for step in pushed]
         part = buf.at[pl.ds(0, count - 1), used]
         pltpu.make_async_copy(part, part, sum_recv.at[r]).wait()
         parts = [buf[i, used] for i in range(count)]

time: 47.1 us -> 46.6 us (0.989)
  Pallas kernels: 46.3 us -> 45.8 us
where the time goes in v6:
time: 46.6 us; the launch traced here: 46.5 us
  Pallas kernels  45.8 us (98%)
  other arithmetic  0.67 us (1%)
    pallas_call x1, Pallas kernels, local(): pl.pallas_call(functools.partial(kernel, (n_row, n_col)), out_shape=pltpu...  45.8 us

profile of v6, /device:TPU:1, one launch (start us, length us, event | category | flops | bytes accessed | tf_op | source)
XLA Modules:
  0.0 46.5 jit_solution(9228666818036300296)
XLA Ops:
  0.0 0.0 copy-start
  0.0 45.8 %transient.1 = f32[2,128,128]{2,1,0:T(8,128)S(1)} custom-call(f32[2,128,128]{2,1,0:T(8,128)} %bitcast.21, f32[2,128,128]{2,1,0:T(8,128)} %bitcast.22, f32[2,128,128]{2,1,0:T(8,128)} %bitcast.23, f32[2,128]{1,0:T(2,128)} %bitcast.29, f32[4,32]{1,0:T(4,128)} %bitcast.28, s32[1,64]{1,0:T(1,128)} %bitcast.30, s32[8,32]{1,0:T(8,128)} %bitcast.24, ...), custom_call_target="tpu_custom_call" | custom-call | tf_op jit(solution)/shard_map/transient/pallas_call | solution.py:589
  45.8 0.0 copy-done
  45.8 0.7 %bitcast_add_fusion = f32[1,2,128,128]{3,2,1,0:T(8,128)} fusion(f32[1,2,128,128]{3,2,1,0:T(8,128)S(1)} %copy-done, f32[2,128,128]{2,1,0:T(8,128)S(1)} %transient.1), kind=kLoop, calls=%fused_computation | loop fusion | flops 32768 | bytes 393216 | tf_op jit(solution)/shard_map/add | solution.py:623
Async XLA Ops:
  0.0 45.8 %copy-start = (f32[1,2,128,128]{3,2,1,0:T(8,128)S(1)}, f32[1,2,128,128]{3,2,1,0:T(8,128)}, u32[]{:S(2)}) copy-start(f32[1,2,128,128]{3,2,1,0:T(8,128)} %param.11) | copy-start | bytes 393220
